TPU v7x, 32 devices: a whole 2x2x4 slice. The times are simulated.
32 devices in a mesh: gx: 2 (over x), gy: 4 (over y, core), gz: 4 (over z).
Axes of the slice: x: 2, y: 2, z: 4, core: 2. Of those that a mesh axis runs over, the one named last changes fastest.
Arguments:
- displacement: float32 [3, 64, 128, 512], P(None, 'gz', 'gx', 'gy'), may hold values from -6 to 6
- pressure: float32 [64, 128, 512], P('gz', 'gx', 'gy'), may hold values from -6 to 6
- zone: int32 [64, 128, 512], P('gz', 'gx', 'gy'), may hold values from 0 to 7
- perm_table: float32 [8], replicated, may hold values from 0.2 to 5
- thickness: int32 [128, 512], P('gx', 'gy'), may hold values from 1 to 64, as said below
Outputs:
- heights: float32 [64, 128, 512], P('gz', 'gx', 'gy')
- flow_residual: float32 [64, 128, 512], P('gz', 'gx', 'gy')
- mech_residual: float32 [3, 64, 128, 512], P(None, 'gz', 'gx', 'gy')
Inputs may be any that keep to these rules, and one draw needn't show every extreme that they name: Every draw has a column of thickness 64; a rectangular region of the lateral plane holds thick deposit, the rest thin deposit.
All inputs are finite; a program needn't handle non-finite values.
Results may differ from a plain program's by a relative error of at most 0.00002.
Values sent between devices are 32-bit elements; how exact they have to be, the bound alone decides.
A program may use at most 64 MiB of HBM per device.

v0:
```python
import jax
import jax.numpy as jnp
from jax import lax
from jax.sharding import PartitionSpec as P

ZONES = 8


def padded(block, sides, width):
    for axis, dim in sides:
        count = lax.axis_size(axis)
        forward = [(i, i + 1) for i in range(count - 1)]
        backward = [(target, source) for source, target in forward]
        low = lax.ppermute(
            lax.slice_in_dim(block, block.shape[dim] - width, None, axis=dim), axis, forward
        )
        high = lax.ppermute(lax.slice_in_dim(block, 0, width, axis=dim), axis, backward)
        block = jnp.concatenate([low, block, high], axis=dim)
    return block


def take(field, dz, dx, dy):
    return field[
        ...,
        1 + dz : field.shape[-3] - 1 + dz,
        1 + dx : field.shape[-2] - 1 + dx,
        1 + dy : field.shape[-1] - 1 + dy,
    ]


def strain_of(disp_pad):
    div = 0.5 * (take(disp_pad[0], 0, 1, 0) - take(disp_pad[0], 0, -1, 0))
    div = div + 0.5 * (take(disp_pad[1], 0, 0, 1) - take(disp_pad[1], 0, 0, -1))
    div = div + 0.5 * (take(disp_pad[2], 1, 0, 0) - take(disp_pad[2], -1, 0, 0))
    return 0.3 * jnp.tanh(div)


def stencils(disp_pad, press_pad, strain_pad, perm_pad):
    press_mid = take(press_pad, 0, 0, 0)
    perm_mid = take(perm_pad, 0, 0, 0)
    strain_mid = take(strain_pad, 0, 0, 0)
    height_mid = 1.0 + strain_mid
    flow = jnp.zeros_like(press_mid)
    for dz, dx, dy in ((1, 0, 0), (-1, 0, 0), (0, 1, 0), (0, -1, 0), (0, 0, 1), (0, 0, -1)):
        perm_nb = take(perm_pad, dz, dx, dy)
        if dz == 0:
            cond = 2.0 * perm_mid * perm_nb / (perm_mid + perm_nb)
        else:
            height_nb = 1.0 + take(strain_pad, dz, dx, dy)
            cond = 4.0 * perm_mid * perm_nb / ((perm_mid + perm_nb) * (height_mid + height_nb))
        flow = flow + cond * (take(press_pad, dz, dx, dy) - press_mid)
    flow = flow - strain_mid
    disp_mid = take(disp_pad, 0, 0, 0)
    lateral = (
        take(disp_pad, 0, 1, 0)
        + take(disp_pad, 0, -1, 0)
        + take(disp_pad, 0, 0, 1)
        + take(disp_pad, 0, 0, -1)
        - 4.0 * disp_mid
    )
    height_up = 1.0 + take(strain_pad, 1, 0, 0)
    height_dn = 1.0 + take(strain_pad, -1, 0, 0)
    vertical = 2.0 * (take(disp_pad, 1, 0, 0) - disp_mid) / (height_mid + height_up) - 2.0 * (
        disp_mid - take(disp_pad, -1, 0, 0)
    ) / (height_mid + height_dn)

    def grads(field):
        return jnp.stack(
            [
                0.5 * (take(field, 0, 1, 0) - take(field, 0, -1, 0)),
                0.5 * (take(field, 0, 0, 1) - take(field, 0, 0, -1)),
                0.5 * (take(field, 1, 0, 0) - take(field, -1, 0, 0)),
            ]
        )

    mech = lateral + vertical + 0.5 * grads(strain_pad) - grads(press_pad)
    return (flow, mech)


def column_sums(column_local):
    pieces = lax.all_gather(column_local[None], "gz", axis=0, tiled=True)
    below = (jnp.arange(pieces.shape[0], dtype=jnp.int32) < lax.axis_index("gz")).astype(
        jnp.float32
    )
    offset = jnp.sum(pieces * below[:, None, None], axis=0)
    total = jnp.sum(pieces, axis=0)
    return (offset, total)


def zone_lookup(zone_field, perm_table, match_dtype):
    zone_perm = jnp.zeros(zone_field.shape, jnp.float32)
    for index in range(ZONES):
        zone_perm = zone_perm + jnp.where(
            zone_field == jnp.asarray(index, match_dtype), perm_table[index], jnp.float32(0.0)
        )
    return zone_perm


def local(displacement, pressure, zone, perm_table, thickness):
    depth_local = displacement.shape[1]
    depth_total = depth_local * lax.axis_size("gz")
    disp_pad = padded(displacement, (("gx", 2), ("gy", 3), ("gz", 1)), 1)
    strain = strain_of(disp_pad)
    layer = (
        lax.axis_index("gz") * depth_local + jnp.arange(depth_local, dtype=jnp.int32)[:, None, None]
    )
    active = (layer < thickness[None, :, :]).astype(jnp.float32)
    cell_thick = (1.0 + strain) * active
    local_prefix = jnp.cumsum(cell_thick, axis=0)
    offset, total = column_sums(local_prefix[-1])
    prefix = local_prefix + offset[None, :, :]
    heights = prefix / depth_total
    burden = (total[None, :, :] - prefix) / depth_total
    zone_perm = zone_lookup(zone, perm_table, jnp.int32)
    kperm = zone_perm * (1.0 + strain) ** 3 / (1.0 + 2.0 * burden) * (0.001 + 0.999 * active)
    state = jnp.stack([pressure, strain, kperm])
    state_pad = padded(state, (("gx", 2), ("gy", 3), ("gz", 1)), 1)
    flow, mech = stencils(disp_pad, state_pad[0], state_pad[1], state_pad[2])
    return (heights, flow, mech)


def solution(mesh):
    in_specs = (
        P(None, "gz", "gx", "gy"),
        P("gz", "gx", "gy"),
        P("gz", "gx", "gy"),
        P(),
        P("gx", "gy"),
    )
    out_specs = (P("gz", "gx", "gy"), P("gz", "gx", "gy"), P(None, "gz", "gx", "gy"))
    return jax.shard_map(local, mesh=mesh, in_specs=in_specs, out_specs=out_specs, check_vma=False)
```

profile of v0, /device:TPU:0, one launch (start us, length us, event | category | flops | bytes accessed | tf_op | source)
XLA Modules:
  0.0 115.6 jit_solution(5458774928147168)
XLA Ops:
  1.7 4.8 %collective-permute-start = (f32[3,16,1,128]{3,2,1,0:T(1,128)S(1)}, f32[3,16,1,128]{3,2,1,0:T(1,128)S(1)}, u32[]{:S(2)}, u32[]{:S(2)}) collective-permute-start(f32[3,16,1,128]{3,2,1,0:T(1,128)S(1)} %get-tuple-element.24), channel_id=1, source_target_pairs={{0,16},{1,17},{2,18},{3,19},{4,20},{5,21},{6,22},{7,23},{8,24},{9,... | collective-permute-start | bytes 73736 | tf_op jit(solution)/shard_map/ppermute | solution.py:14
  7.8 1.6 %fusion.46 = (f32[1]{0:T(128)}, f32[1]{0:T(128)}, f32[1]{0:T(128)}, f32[1]{0:T(128)}, f32[1]{0:T(128)}, /*index=5*/f32[1]{0:T(128)}, f32[1]{0:T(128)}, f32[1]{0:T(128)}) fusion(f32[8]{0:T(128)} %param.8), kind=kLoop, calls=%fused_computation.112 | loop fusion | bytes 64 | tf_op jit(solution)/shard_map/slice | solution.py:94
  9.5 2.8 %collective-permute-done.1 = f32[3,16,1,128]{3,2,1,0:T(1,128)S(1)} collective-permute-done((f32[3,16,1,128]{3,2,1,0:T(1,128)S(1)}, f32[3,16,1,128]{3,2,1,0:T(1,128)S(1)}, u32[]{:S(2)}, u32[]{:S(2)}) %collective-permute-start.1) | collective-permute-done | bytes 24608 | tf_op jit(solution)/shard_map/ppermute | solution.py:17
  18.2 3.0 %collective-permute-start.2 = (f32[3,16,66,1]{2,1,3,0:T(8,128)S(1)}, f32[3,16,66,1]{2,1,3,0:T(8,128)S(1)}, u32[]{:S(2)}, u32[]{:S(2)}) collective-permute-start(f32[3,16,66,1]{2,1,3,0:T(8,128)S(1)} %copy-done.26), channel_id=1, source_target_pairs={{0,4},{4,8},{8,12},{1,5},{5,9},{9,13},{2,6},{6,10},{10,14},{3,7},{... | collective-permute-start | bytes 38024 | tf_op jit(solution)/shard_map/ppermute | solution.py:14
  25.6 3.5 %collective-permute-start.4 = (f32[3,1,66,130]{3,2,1,0:T(8,128)S(1)}, f32[3,1,66,130]{3,2,1,0:T(8,128)S(1)}, u32[]{:S(2)}, u32[]{:S(2)}) collective-permute-start(f32[3,1,66,130]{3,2,1,0:T(8,128)S(1)} %get-tuple-element.10), channel_id=1, source_target_pairs={{0,1},{1,2},{2,3},{4,5},{5,6},{6,7},{8,9},{9,10},{10,11},{12,13},{... | collective-permute-start | bytes 308888 | tf_op jit(solution)/shard_map/ppermute | solution.py:14
  30.5 4.2 %collective-permute-done.4 = f32[3,1,66,130]{3,2,1,0:T(8,128)S(1)} collective-permute-done((f32[3,1,66,130]{3,2,1,0:T(8,128)S(1)}, f32[3,1,66,130]{3,2,1,0:T(8,128)S(1)}, u32[]{:S(2)}, u32[]{:S(2)}) %collective-permute-start.4) | collective-permute-done | bytes 102992 | tf_op jit(solution)/shard_map/ppermute | solution.py:14
  34.7 4.7 %collective-permute-done.5 = f32[3,1,66,130]{3,2,1,0:T(8,128)S(1)} collective-permute-done((f32[3,1,66,130]{3,2,1,0:T(8,128)S(1)}, f32[3,1,66,130]{3,2,1,0:T(8,128)S(1)}, u32[]{:S(2)}, u32[]{:S(2)}) %collective-permute-start.5) | collective-permute-done | bytes 102992 | tf_op jit(solution)/shard_map/ppermute | solution.py:17
  40.0 2.8 %pad_maximum_fusion = f32[3,18,66,130]{3,2,1,0:T(8,128)S(1)} fusion(f32[3,1,66,130]{3,2,1,0:T(8,128)S(1)} %collective-permute-done.5, f32[3,16,66,1]{3,2,1,0:T(8,128)S(1)} %copy.11, f32[3,16,1,128]{3,2,1,0:T(1,128)S(1)} %copy-done.19, f32[3,16,64,128]{3,2,1,0:T(8,128)S(1)} %copy-done.2, f32[3,16,1,128]{3,2,1,0:T(1,128)S(1)} %copy-done.16, ...), kind=kLoop, calls=%fused_computation | loop fusion | flops 2779920 | bytes 3706560 | tf_op jit(solution)/shard_map/concatenate | solution.py:18
  44.2 13.7 %all_gather.3 = f32[4,64,128]{2,1,0:T(8,128)S(1)} all-gather(f32[1,64,128]{2,1,0:T(8,128)S(1)} %slice.270), channel_id=1, replica_groups=mesh['gx'=2,'gy'=4,'gz'=4] {'gz'}, dimensions={0}, use_global_device_ids=true | all-gather | bytes 163840 | tf_op jit(solution)/shard_map/all_gather | solution.py:81
  58.0 6.3 %fusion.17 = (f32[1,16,64,128]{3,2,1,0:T(8,128)S(1)}, f32[16,64,128]{2,1,0:T(8,128)}) fusion(s32[16,64,128]{2,1,0:T(8,128)S(1)} %copy-done.14, f32[16,64,128]{2,1,0:T(8,128)S(1)} %fusion.14, f32[16,64,128]{2,1,0:T(8,128)S(1)} %fusion.27, f32[64,128]{1,0:T(8,128)S(1)} %get-tuple-element.3, f32[]{:T(128)} %bitcast.12, f32[]{:T(128)} %bitcast.11, f32[]{:T(128)} %bitcast.10, ...), kind=kLoop, calls=%fused_computation.49 | loop fusion | flops 4849664 | bytes 2719840 | tf_op jit(solution)/shard_map/stack | solution.py:116
  64.3 2.3 %collective-permute-start.6 = (f32[3,16,1,128]{3,2,1,0:T(1,128)S(1)}, f32[3,16,1,128]{3,2,1,0:T(1,128)S(1)}, u32[]{:S(2)}, u32[]{:S(2)}) collective-permute-start(f32[3,16,1,128]{3,2,1,0:T(1,128)S(1)} %get-tuple-element.22), channel_id=1, source_target_pairs={{0,16},{1,17},{2,18},{3,19},{4,20},{5,21},{6,22},{7,23},{8,24},{9,... | collective-permute-start | bytes 73736 | tf_op jit(solution)/shard_map/ppermute | solution.py:14
  68.2 4.2 %collective-permute-done.7 = f32[3,16,1,128]{3,2,1,0:T(1,128)S(1)} collective-permute-done((f32[3,16,1,128]{3,2,1,0:T(1,128)S(1)}, f32[3,16,1,128]{3,2,1,0:T(1,128)S(1)}, u32[]{:S(2)}, u32[]{:S(2)}) %collective-permute-start.7) | collective-permute-done | bytes 24608 | tf_op jit(solution)/shard_map/ppermute | solution.py:17
  73.3 2.3 %fusion.43 = (f32[3,16,66,1]{3,2,1,0:T(8,128)}, f32[3,16,66,1]{3,2,1,0:T(8,128)}) fusion(f32[3,16,66,128]{3,2,1,0:T(8,128)S(1)} %pad_maximum_fusion.3), kind=kLoop, calls=%fused_computation.109 | loop fusion | bytes 50688 | tf_op jit(solution)/shard_map/slice | solution.py:15
  75.6 2.7 %copy.12 = f32[3,16,66,1]{2,1,3,0:T(8,128)} copy(f32[3,16,66,1]{3,2,1,0:T(8,128)} %get-tuple-element.18) | data formatting | bytes 25344 | tf_op jit(solution)/shard_map/slice | solution.py:15
  78.3 1.9 %collective-permute-start.8 = (f32[3,16,66,1]{2,1,3,0:T(8,128)}, f32[3,16,66,1]{2,1,3,0:T(8,128)}, u32[]{:S(2)}, u32[]{:S(2)}) collective-permute-start(f32[3,16,66,1]{2,1,3,0:T(8,128)} %copy.12), channel_id=1, source_target_pairs={{0,4},{4,8},{8,12},{1,5},{5,9},{9,13},{2,6},{6,10},{10,14},{3,7},{... | collective-permute-start | bytes 38024 | tf_op jit(solution)/shard_map/ppermute | solution.py:14
  80.1 2.7 %copy.13 = f32[3,16,66,1]{2,1,3,0:T(8,128)} copy(f32[3,16,66,1]{3,2,1,0:T(8,128)} %get-tuple-element.19) | data formatting | bytes 25344 | tf_op jit(solution)/shard_map/slice | solution.py:17
  84.1 2.6 %copy.14 = f32[3,16,66,1]{3,2,1,0:T(8,128)} copy(f32[3,16,66,1]{2,1,3,0:T(8,128)} %collective-permute-done.8) | data formatting | bytes 25344 | tf_op jit(solution)/shard_map/ppermute | solution.py:14
  87.1 2.6 %copy.15 = f32[3,16,66,1]{3,2,1,0:T(8,128)} copy(f32[3,16,66,1]{2,1,3,0:T(8,128)} %collective-permute-done.9) | data formatting | bytes 25344 | tf_op jit(solution)/shard_map/ppermute | solution.py:17
  91.3 1.9 %collective-permute-start.10 = (f32[3,1,66,130]{3,2,1,0:T(8,128)S(1)}, f32[3,1,66,130]{3,2,1,0:T(8,128)S(1)}, u32[]{:S(2)}, u32[]{:S(2)}) collective-permute-start(f32[3,1,66,130]{3,2,1,0:T(8,128)S(1)} %get-tuple-element.8), channel_id=1, source_target_pairs={{0,1},{1,2},{2,3},{4,5},{5,6},{6,7},{8,9},{9,10},{10,11},{12,13},{... | collective-permute-start | bytes 308888 | tf_op jit(solution)/shard_map/ppermute | solution.py:14
  94.7 2.7 %collective-permute-done.10 = f32[3,1,66,130]{3,2,1,0:T(8,128)S(1)} collective-permute-done((f32[3,1,66,130]{3,2,1,0:T(8,128)S(1)}, f32[3,1,66,130]{3,2,1,0:T(8,128)S(1)}, u32[]{:S(2)}, u32[]{:S(2)}) %collective-permute-start.10) | collective-permute-done | bytes 102992 | tf_op jit(solution)/shard_map/ppermute | solution.py:14
  97.3 4.7 %collective-permute-done.11 = f32[3,1,66,130]{3,2,1,0:T(8,128)S(1)} collective-permute-done((f32[3,1,66,130]{3,2,1,0:T(8,128)S(1)}, f32[3,1,66,130]{3,2,1,0:T(8,128)S(1)}, u32[]{:S(2)}, u32[]{:S(2)}) %collective-permute-start.11) | collective-permute-done | bytes 102992 | tf_op jit(solution)/shard_map/ppermute | solution.py:17
  102.1 3.6 %pad_maximum_fusion.1 = f32[3,18,66,130]{3,2,1,0:T(8,128)S(1)} fusion(f32[3,1,66,130]{3,2,1,0:T(8,128)S(1)} %collective-permute-done.11, f32[3,16,66,1]{3,2,1,0:T(8,128)S(1)} %copy-done.5, f32[3,16,1,128]{3,2,1,0:T(1,128)S(1)} %copy-done.24, f32[1,16,64,128]{3,2,1,0:T(8,128)S(1)} %copy-done.7, f32[1,16,64,128]{3,2,1,0:T(8,128)S(1)} %bitcast.39, ...), kind=kLoop, calls=%fused_computation.1 | loop fusion | flops 3706560 | bytes 3706560 | tf_op jit(solution)/shard_map/concatenate | solution.py:18
  107.5 2.9 %add_subtract_fusion = (f32[16,64,128]{2,1,0:T(8,128)}, f32[16,64,128]{2,1,0:T(8,128)S(1)}, f32[16,64,128]{2,1,0:T(8,128)S(1)}) fusion(f32[18,66,130]{2,1,0:T(8,128)S(1)} %get-tuple-element.14, f32[18,66,130]{2,1,0:T(8,128)S(1)} %get-tuple-element.13, f32[18,66,130]{2,1,0:T(8,128)S(1)} %get-tuple-element.12), kind=kLoop, calls=%fused_computation.70 | loop fusion | flops 5898240 | bytes 10485760 | tf_op jit(solution)/shard_map/sub | solution.py:52
  110.4 5.2 %fusion.6 = f32[3,16,64,128]{3,2,1,0:T(8,128)} fusion(f32[3,16,64,128]{3,2,1,0:T(8,128)S(1)} %copy-done.3, f32[3,1,66,130]{3,2,1,0:T(8,128)S(1)} %copy-done.11, f32[3,16,66,1]{3,2,1,0:T(8,128)S(1)} %copy.11, f32[3,16,66,1]{3,2,1,0:T(8,128)S(1)} %copy.10, f32[3,16,1,128]{3,2,1,0:T(1,128)S(1)} %copy-done.20, f32[3,16,1,128]{3,2,1,0:T(1,128)S(1)} %copy-done.17, ...), kind=kLoop, calls=%fused_computation.11 | loop fusion | flops 14942208 | bytes 7620448 | tf_op jit(solution)/shard_map/sub | solution.py:76
  (86 shorter events, 24.7 us)
Async XLA Ops:
  1.7 7.8 %collective-permute-start = (f32[3,16,1,128]{3,2,1,0:T(1,128)S(1)}, f32[3,16,1,128]{3,2,1,0:T(1,128)S(1)}, u32[]{:S(2)}, u32[]{:S(2)}) collective-permute-start(f32[3,16,1,128]{3,2,1,0:T(1,128)S(1)} %get-tuple-element.24), channel_id=1, source_target_pairs={{0,16},{1,17},{2,18},{3,19},{4,20},{5,21},{6,22},{7,23},{8,24},{9,... | collective-permute-start | bytes 73736 | tf_op jit(solution)/shard_map/ppermute | solution.py:14
  6.5 5.7 %collective-permute-start.1 = (f32[3,16,1,128]{3,2,1,0:T(1,128)S(1)}, f32[3,16,1,128]{3,2,1,0:T(1,128)S(1)}, u32[]{:S(2)}, u32[]{:S(2)}) collective-permute-start(f32[3,16,1,128]{3,2,1,0:T(1,128)S(1)} %get-tuple-element.25), channel_id=1, source_target_pairs={{16,0},{17,1},{18,2},{19,3},{20,4},{21,5},{22,6},{23,7},{24,8},{25... | collective-permute-start | bytes 73736 | tf_op jit(solution)/shard_map/ppermute | solution.py:17
  16.9 5.9 %collective-permute-start.3 = (f32[3,16,66,1]{2,1,3,0:T(8,128)S(1)}, f32[3,16,66,1]{2,1,3,0:T(8,128)}, u32[]{:S(2)}, u32[]{:S(2)}) collective-permute-start(f32[3,16,66,1]{2,1,3,0:T(8,128)S(1)} %copy.9), channel_id=1, source_target_pairs={{4,0},{8,4},{12,8},{5,1},{9,5},{13,9},{6,2},{10,6},{14,10},{7,3},{... | collective-permute-start | bytes 38024 | tf_op jit(solution)/shard_map/ppermute | solution.py:17
  18.2 3.9 %collective-permute-start.2 = (f32[3,16,66,1]{2,1,3,0:T(8,128)S(1)}, f32[3,16,66,1]{2,1,3,0:T(8,128)S(1)}, u32[]{:S(2)}, u32[]{:S(2)}) collective-permute-start(f32[3,16,66,1]{2,1,3,0:T(8,128)S(1)} %copy-done.26), channel_id=1, source_target_pairs={{0,4},{4,8},{8,12},{1,5},{5,9},{9,13},{2,6},{6,10},{10,14},{3,7},{... | collective-permute-start | bytes 38024 | tf_op jit(solution)/shard_map/ppermute | solution.py:14
  24.3 15.7 %copy-start.2 = (f32[3,16,64,128]{3,2,1,0:T(8,128)S(1)}, f32[3,16,64,128]{3,2,1,0:T(8,128)}, u32[]{:S(2)}) copy-start(f32[3,16,64,128]{3,2,1,0:T(8,128)} %param.5) | copy-start | bytes 4718596
  24.3 15.7 %copy-start.16 = (f32[3,16,1,128]{3,2,1,0:T(1,128)S(1)}, f32[3,16,1,128]{3,2,1,0:T(1,128)}, u32[]{:S(2)}) copy-start(f32[3,16,1,128]{3,2,1,0:T(1,128)} %copy-done.15) | copy-start | bytes 73732
  24.3 15.7 %copy-start.19 = (f32[3,16,1,128]{3,2,1,0:T(1,128)S(1)}, f32[3,16,1,128]{3,2,1,0:T(1,128)}, u32[]{:S(2)}) copy-start(f32[3,16,1,128]{3,2,1,0:T(1,128)} %copy-done.18) | copy-start | bytes 73732
  25.6 9.0 %collective-permute-start.4 = (f32[3,1,66,130]{3,2,1,0:T(8,128)S(1)}, f32[3,1,66,130]{3,2,1,0:T(8,128)S(1)}, u32[]{:S(2)}, u32[]{:S(2)}) collective-permute-start(f32[3,1,66,130]{3,2,1,0:T(8,128)S(1)} %get-tuple-element.10), channel_id=1, source_target_pairs={{0,1},{1,2},{2,3},{4,5},{5,6},{6,7},{8,9},{9,10},{10,11},{12,13},{... | collective-permute-start | bytes 308888 | tf_op jit(solution)/shard_map/ppermute | solution.py:14
  29.1 10.2 %collective-permute-start.5 = (f32[3,1,66,130]{3,2,1,0:T(8,128)S(1)}, f32[3,1,66,130]{3,2,1,0:T(8,128)S(1)}, u32[]{:S(2)}, u32[]{:S(2)}) collective-permute-start(f32[3,1,66,130]{3,2,1,0:T(8,128)S(1)} %get-tuple-element.11), channel_id=1, source_target_pairs={{1,0},{2,1},{3,2},{5,4},{6,5},{7,6},{9,8},{10,9},{11,10},{13,12},{... | collective-permute-start | bytes 308888 | tf_op jit(solution)/shard_map/ppermute | solution.py:17
  44.0 28.4 %copy-start = (f32[16,64,128]{2,1,0:T(8,128)}, f32[16,64,128]{2,1,0:T(8,128)S(1)}, u32[]{:S(2)}) copy-start(f32[16,64,128]{2,1,0:T(8,128)S(1)} %fusion.27) | copy-start | bytes 1572868
  44.0 13.9 %copy-start.14 = (s32[16,64,128]{2,1,0:T(8,128)S(1)}, s32[16,64,128]{2,1,0:T(8,128)}, u32[]{:S(2)}) copy-start(s32[16,64,128]{2,1,0:T(8,128)} %param.7) | copy-start | bytes 1572868
  44.2 20.1 %copy-start.8 = (f32[16,64,128]{2,1,0:T(8,128)S(1)}, f32[16,64,128]{2,1,0:T(8,128)}, u32[]{:S(2)}) copy-start(f32[16,64,128]{2,1,0:T(8,128)} %param.6) | copy-start | bytes 1572868
  64.3 3.9 %collective-permute-start.6 = (f32[3,16,1,128]{3,2,1,0:T(1,128)S(1)}, f32[3,16,1,128]{3,2,1,0:T(1,128)S(1)}, u32[]{:S(2)}, u32[]{:S(2)}) collective-permute-start(f32[3,16,1,128]{3,2,1,0:T(1,128)S(1)} %get-tuple-element.22), channel_id=1, source_target_pairs={{0,16},{1,17},{2,18},{3,19},{4,20},{5,21},{6,22},{7,23},{8,24},{9,... | collective-permute-start | bytes 73736 | tf_op jit(solution)/shard_map/ppermute | solution.py:14
  66.7 5.7 %collective-permute-start.7 = (f32[3,16,1,128]{3,2,1,0:T(1,128)S(1)}, f32[3,16,1,128]{3,2,1,0:T(1,128)S(1)}, u32[]{:S(2)}, u32[]{:S(2)}) collective-permute-start(f32[3,16,1,128]{3,2,1,0:T(1,128)S(1)} %get-tuple-element.23), channel_id=1, source_target_pairs={{16,0},{17,1},{18,2},{19,3},{20,4},{21,5},{22,6},{23,7},{24,8},{25... | collective-permute-start | bytes 73736 | tf_op jit(solution)/shard_map/ppermute | solution.py:17
  78.3 5.9 %collective-permute-start.8 = (f32[3,16,66,1]{2,1,3,0:T(8,128)}, f32[3,16,66,1]{2,1,3,0:T(8,128)}, u32[]{:S(2)}, u32[]{:S(2)}) collective-permute-start(f32[3,16,66,1]{2,1,3,0:T(8,128)} %copy.12), channel_id=1, source_target_pairs={{0,4},{4,8},{8,12},{1,5},{5,9},{9,13},{2,6},{6,10},{10,14},{3,7},{... | collective-permute-start | bytes 38024 | tf_op jit(solution)/shard_map/ppermute | solution.py:14
  82.8 4.3 %collective-permute-start.9 = (f32[3,16,66,1]{2,1,3,0:T(8,128)}, f32[3,16,66,1]{2,1,3,0:T(8,128)}, u32[]{:S(2)}, u32[]{:S(2)}) collective-permute-start(f32[3,16,66,1]{2,1,3,0:T(8,128)} %copy.13), channel_id=1, source_target_pairs={{4,0},{8,4},{12,8},{5,1},{9,5},{13,9},{6,2},{10,6},{14,10},{7,3},{... | collective-permute-start | bytes 38024 | tf_op jit(solution)/shard_map/ppermute | solution.py:17
  89.7 12.3 %copy-start.4 = (f32[3,16,66,1]{3,2,1,0:T(8,128)S(1)}, f32[3,16,66,1]{3,2,1,0:T(8,128)}, u32[]{:S(2)}) copy-start(f32[3,16,66,1]{3,2,1,0:T(8,128)} %copy.14) | copy-start | bytes 38020
  89.7 12.3 %copy-start.5 = (f32[3,16,66,1]{3,2,1,0:T(8,128)S(1)}, f32[3,16,66,1]{3,2,1,0:T(8,128)}, u32[]{:S(2)}) copy-start(f32[3,16,66,1]{3,2,1,0:T(8,128)} %copy.15) | copy-start | bytes 38020
  89.7 12.3 %copy-start.7 = (f32[1,16,64,128]{3,2,1,0:T(8,128)S(1)}, f32[1,16,64,128]{3,2,1,0:T(8,128)}, u32[]{:S(2)}) copy-start(f32[1,16,64,128]{3,2,1,0:T(8,128)} %copy-done.6) | copy-start | bytes 1572868
  89.7 12.3 %copy-start.9 = (f32[16,64,128]{2,1,0:T(8,128)S(1)}, f32[16,64,128]{2,1,0:T(8,128)}, u32[]{:S(2)}) copy-start(f32[16,64,128]{2,1,0:T(8,128)} %param.6) | copy-start | bytes 1572868
  89.8 12.3 %copy-start.22 = (f32[3,16,1,128]{3,2,1,0:T(1,128)S(1)}, f32[3,16,1,128]{3,2,1,0:T(1,128)}, u32[]{:S(2)}) copy-start(f32[3,16,1,128]{3,2,1,0:T(1,128)} %copy-done.21) | copy-start | bytes 73732
  89.8 12.3 %copy-start.24 = (f32[3,16,1,128]{3,2,1,0:T(1,128)S(1)}, f32[3,16,1,128]{3,2,1,0:T(1,128)}, u32[]{:S(2)}) copy-start(f32[3,16,1,128]{3,2,1,0:T(1,128)} %copy-done.23) | copy-start | bytes 73732
  91.3 6.1 %collective-permute-start.10 = (f32[3,1,66,130]{3,2,1,0:T(8,128)S(1)}, f32[3,1,66,130]{3,2,1,0:T(8,128)S(1)}, u32[]{:S(2)}, u32[]{:S(2)}) collective-permute-start(f32[3,1,66,130]{3,2,1,0:T(8,128)S(1)} %get-tuple-element.8), channel_id=1, source_target_pairs={{0,1},{1,2},{2,3},{4,5},{5,6},{6,7},{8,9},{9,10},{10,11},{12,13},{... | collective-permute-start | bytes 308888 | tf_op jit(solution)/shard_map/ppermute | solution.py:14
  93.2 8.9 %collective-permute-start.11 = (f32[3,1,66,130]{3,2,1,0:T(8,128)S(1)}, f32[3,1,66,130]{3,2,1,0:T(8,128)S(1)}, u32[]{:S(2)}, u32[]{:S(2)}) collective-permute-start(f32[3,1,66,130]{3,2,1,0:T(8,128)S(1)} %get-tuple-element.9), channel_id=1, source_target_pairs={{1,0},{2,1},{3,2},{5,4},{6,5},{7,6},{9,8},{10,9},{11,10},{13,12},{... | collective-permute-start | bytes 308888 | tf_op jit(solution)/shard_map/ppermute | solution.py:17
  (15 other events, 51.4 us)
where the time goes:
time: 117 us; the launch traced here: 116 us
  other arithmetic  27.9 us (24%)
  starting transfers between devices  25.4 us (22%)
  waiting for transfers between devices  24.7 us (21%)
  local copies, waits for them, and re-layouts  22.8 us (19%)
  blocking collectives  13.7 us (12%)
    ppermute x6, starting transfers between devices, padded(): lax.ppermute(lax.slice_in_dim(block, block.shape[dim] - width, None, axis...  17.5 us
    ppermute x6, waiting for transfers between devices, padded(): lax.ppermute(lax.slice_in_dim(block, 0, width, axis=dim), axis, backward)  16.8 us
    all_gather x1, blocking collectives, column_sums(): pieces = lax.all_gather(column_local[None], 'gz', axis=0, tiled=True)  13.7 us
    concatenate x4, other arithmetic, padded(): block = jnp.concatenate([low, block, high], axis=dim)  8.24 us
    ppermute x6, starting transfers between devices, padded(): lax.ppermute(lax.slice_in_dim(block, 0, width, axis=dim), axis, backward)  7.93 us
    ppermute x6, waiting for transfers between devices, padded(): lax.ppermute(lax.slice_in_dim(block, block.shape[dim] - width, None, axis...  7.92 us
    slice x5, local copies, waits for them, and re-layouts, padded(): lax.slice_in_dim(block, block.shape[dim] - width, None, axis=dim)  7.87 us
    another operation x1, other arithmetic, local(): state = jnp.stack([pressure, strain, kperm])  6.34 us
  transfers between devices with their start and end apart: 12, of which 9 were waited for; matrix products, arithmetic and copies ran while one was open for 7% of the time, Pallas kernels for 0%

commit v1 on v0

v1 whole, which is shorter than its diff:
```python
import functools

import jax
import jax.numpy as jnp
from jax import lax
from jax.experimental import pallas as pl
from jax.experimental.pallas import tpu as pltpu
from jax.sharding import PartitionSpec as P

MESH = pl.DeviceIdType.MESH
ZONES = 8
AXES = ("gx", "gy", "gz")
PAD = 8
ROWS = 16

X1, Y1, ZU, ZL, ZP, ZN, X2, Y2, ZS, X3, Y3 = range(11)
MESSAGES = 11


def kernel(
    counts, disp, press, zone, table, thick, heights, flow, mech,
    u, p, s, k, zn, th, pre, tot, xs1, xr1, ys1, yr1, xs2, xr2, ys2, yr2, xs3, xr3, ys3, yr3, cs,
    load_sem, send_sem, recv_sem, col_send, col_recv,
):
    depth, width = disp.shape[1], disp.shape[2]
    lanes = disp.shape[3]
    groups = width // 8
    last = PAD + width
    me = {axis: lax.axis_index(axis) for axis in AXES}
    size = dict(zip(AXES, counts))
    depth_total = depth * size["gz"]
    own = pl.ds(PAD, width)
    f32 = jnp.float32

    def has(axis, side):
        return me[axis] > 0 if side == 0 else me[axis] < size[axis] - 1

    def peer(axis, side):
        return {axis: me[axis] + (1 if side else -1)}

    loads = [
        pltpu.make_async_copy(disp.at[1], u.at[1, pl.ds(1, depth), own], load_sem.at[0]),
        pltpu.make_async_copy(disp.at[0], u.at[0, pl.ds(1, depth), own], load_sem.at[1]),
        pltpu.make_async_copy(disp.at[2], u.at[2, pl.ds(1, depth), own], load_sem.at[2]),
        pltpu.make_async_copy(press, p.at[pl.ds(1, depth), own], load_sem.at[3]),
        pltpu.make_async_copy(thick, th, load_sem.at[4]),
        pltpu.make_async_copy(zone, zn.at[pl.ds(1, depth)], load_sem.at[5]),
    ]
    for load in loads:
        load.start()

    barrier = pltpu.get_barrier_semaphore()
    partners = jnp.int32(size["gz"] - 1)
    for axis in ("gx", "gy"):
        for side in (0, 1):
            @pl.when(has(axis, side))
            def _():
                pl.semaphore_signal(barrier, inc=1, device_id=peer(axis, side), device_id_type=MESH)
            partners = partners + has(axis, side).astype(jnp.int32)
    for off in range(1, size["gz"]):
        pl.semaphore_signal(
            barrier, inc=1, device_id={"gz": lax.rem(me["gz"] + off, size["gz"])}, device_id_type=MESH
        )
    pl.semaphore_wait(barrier, partners)

    pending = []

    def copy(message, axis, side, src, dst, at):
        return pltpu.make_async_remote_copy(
            src_ref=src,
            dst_ref=dst,
            send_sem=send_sem.at[message, side],
            recv_sem=recv_sem.at[message, side],
            device_id=peer(axis, at),
            device_id_type=MESH,
        )

    def send(message, axis, srcs, dsts):
        for side in (0, 1):
            @pl.when(has(axis, side))
            def _():
                copy(message, axis, side, srcs[side], dsts[1 - side], side).start()
        pending.append((message, axis, srcs, dsts))

    def receive(message, axis, srcs, dsts):
        for side in (0, 1):
            @pl.when(has(axis, 1 - side))
            def _():
                copy(message, axis, side, srcs[side], dsts[1 - side], 1 - side).wait_recv()

    def clear(axis, refs):
        for side in (0, 1):
            @pl.when(jnp.logical_not(has(axis, side)))
            def _():
                for ref in refs[side]:
                    ref[...] = jnp.zeros(ref.shape, ref.dtype)

    def pair(ref):
        return (ref.at[0], ref.at[1])

    zu = ((disp.at[2, 0], disp.at[2, depth - 1]), (u.at[2, 0, own], u.at[2, depth + 1, own]))
    zl = (
        (disp.at[pl.ds(0, 2), 0], disp.at[pl.ds(0, 2), depth - 1]),
        (u.at[pl.ds(0, 2), 0, own], u.at[pl.ds(0, 2), depth + 1, own]),
    )
    zp = ((press.at[0], press.at[depth - 1]), (p.at[0, own], p.at[depth + 1, own]))
    zz = ((zone.at[0], zone.at[depth - 1]), (zn.at[0], zn.at[depth + 1]))
    zs = ((s.at[1, own], s.at[depth, own]), (s.at[0, own], s.at[depth + 1, own]))
    send(ZU, "gz", *zu)

    lane = lax.broadcasted_iota(jnp.int32, (8, lanes), 1)
    lane_r = lax.broadcasted_iota(jnp.int32, (ROWS, lanes), 1)
    first_lane, last_lane = lane_r == 0, lane_r == lanes - 1
    zero8 = jnp.zeros((8, lanes), f32)

    def pack(values, z, g, lo, hi):
        slot = z * groups + g
        turned = pltpu.roll(values, slot, 1)
        hi = jnp.where(lane == slot, turned, hi)
        lo = jnp.where(lane == lax.rem(slot + lanes - 1, lanes), turned, lo)
        return lo, hi

    def yshift(v, packs, z, row):
        lo, hi = [], []
        lo_pack, hi_pack = packs
        for g in range(ROWS // 8):
            slot = z * groups + row // 8 + g
            lo.append(pltpu.roll(lo_pack, lax.rem(lanes + 1 - slot, lanes), 1))
            hi.append(pltpu.roll(hi_pack, lanes - 1 - slot, 1))
        lo, hi = jnp.concatenate(lo, axis=0), jnp.concatenate(hi, axis=0)
        below = jnp.where(first_lane, lo, pltpu.roll(v, 1, 1))
        above = jnp.where(last_lane, hi, pltpu.roll(v, lanes - 1, 1))
        return below, above

    fields = [u.at[0], u.at[1], u.at[2], p]

    for load in loads[:4]:
        load.wait()

    def pack_inputs(z, accs):
        out = []
        for i, field in enumerate(fields):
            xs1[0, i, z] = field[z + 1, PAD:PAD + 1, :]
            xs1[1, i, z] = field[z + 1, last - 1:last, :]
            lo, hi = accs[2 * i:2 * i + 2]
            for g in range(groups):
                lo, hi = pack(field[z + 1, PAD + 8 * g:PAD + 8 * g + 8, :], z, g, lo, hi)
            out += [lo, hi]
        return tuple(out)

    accs = lax.fori_loop(0, depth, pack_inputs, (zero8,) * 8)
    for i in range(4):
        ys1[0, i] = accs[2 * i + 1]
        ys1[1, i] = accs[2 * i]
    x1, y1 = (pair(xs1), pair(xr1)), (pair(ys1), pair(yr1))
    x2, y2 = (pair(xs2), pair(xr2)), (pair(ys2), pair(yr2))
    x3, y3 = (pair(xs3), pair(xr3)), (pair(ys3), pair(yr3))
    send(X1, "gx", *x1)
    send(Y1, "gy", *y1)
    send(ZL, "gz", *zl)
    send(ZP, "gz", *zp)
    send(ZN, "gz", *zz)

    clear("gx", [[xr.at[side] for xr in (xr1, xr2, xr3)] for side in (0, 1)])
    clear("gy", [[yr.at[side] for yr in (yr1, yr2, yr3)] for side in (0, 1)])
    edges = (0, depth + 1)
    clear("gz", [[u.at[:, z, own], p.at[z, own], s.at[z, own], k.at[z, own], zn.at[z]] for z in edges])
    loads[4].wait()

    receive(ZU, "gz", *zu)
    receive(X1, "gx", *x1)
    receive(Y1, "gy", *y1)

    def unpack_inputs(z, carry):
        for i, field in enumerate(fields):
            field[z + 1, PAD - 1:PAD, :] = xr1[0, i, z]
            field[z + 1, last:last + 1, :] = xr1[1, i, z]
        return carry

    lax.fori_loop(0, depth, unpack_inputs, 0)

    def shifts(field, packs, z, row):
        at = PAD + row
        mid = field[z + 1, at:at + ROWS, :]
        xm = field[z + 1, at - 1:at - 1 + ROWS, :]
        xp = field[z + 1, at + 1:at + 1 + ROWS, :]
        ym, yp = yshift(mid, packs, z, row)
        return mid, xm, xp, ym, yp

    base = me["gz"] * depth
    chunks = range(0, width, ROWS)

    ylo, yhi = zero8, zero8
    for row in chunks:
        rows = slice(row, row + ROWS)
        at = slice(PAD + row, PAD + row + ROWS)
        height = th[rows, :]
        packs = (yr1[0, 1], yr1[1, 1])

        def strain_step(z, carry):
            acc, lo, hi = carry
            up = u[0, z + 1, PAD + row + 1:PAD + row + 1 + ROWS, :]
            down = u[0, z + 1, PAD + row - 1:PAD + row - 1 + ROWS, :]
            ym, yp = yshift(u[1, z + 1, at, :], packs, z, row)
            div = 0.5 * (up - down) + 0.5 * (yp - ym) + 0.5 * (u[2, z + 2, at, :] - u[2, z, at, :])
            st = 0.3 * jnp.tanh(div)
            s[z + 1, at, :] = st
            if row == 0:
                xs2[0, z] = st[0:1, :]
            if row + ROWS == width:
                xs2[1, z] = st[ROWS - 1:ROWS, :]
            for g in range(ROWS // 8):
                lo, hi = pack(st[8 * g:8 * g + 8, :], z, row // 8 + g, lo, hi)
            acc = acc + jnp.where(base + z < height, 1.0 + st, 0.0)
            pre[z, rows, :] = acc
            return acc, lo, hi

        acc, ylo, yhi = lax.fori_loop(0, depth, strain_step, (jnp.zeros((ROWS, lanes), f32), ylo, yhi))
        tot[rows, :] = acc
    ys2[0], ys2[1] = yhi, ylo

    def column(off, at):
        return pltpu.make_async_remote_copy(
            src_ref=tot,
            dst_ref=cs.at[off - 1],
            send_sem=col_send.at[off - 1],
            recv_sem=col_recv.at[off - 1],
            device_id={"gz": lax.rem(me["gz"] + at, size["gz"])},
            device_id_type=MESH,
        )

    for off in range(1, size["gz"]):
        column(off, off).start()
    send(X2, "gx", *x2)
    send(Y2, "gy", *y2)
    send(ZS, "gz", *zs)

    receive(ZP, "gz", *zp)
    for row in chunks:
        rows = slice(row, row + ROWS)
        at = slice(PAD + row, PAD + row + ROWS)
        packs = [(yr1[0, i], yr1[1, i]) for i in range(4)]

        def lateral_step(z, carry):
            _, xm, xp, ym, yp = shifts(p, packs[3], z, row)
            grads = (xp - xm, yp - ym, p[z + 2, at, :] - p[z, at, :])
            for c in range(3):
                mid, xm, xp, ym, yp = shifts(u.at[c], packs[c], z, row)
                mech[c, z, rows, :] = xp + xm + yp + ym - 4.0 * mid - 0.5 * grads[c]
            return carry

        lax.fori_loop(0, depth, lateral_step, 0)

    loads[5].wait()
    for off in range(1, size["gz"]):
        column(off, size["gz"] - off).wait_recv()
    receive(ZS, "gz", *zs)
    receive(ZN, "gz", *zz)

    def permeability(zones, st, burden, active):
        h = 1.0 + st
        perm = jnp.full(zones.shape, table[0], f32)
        for i in range(1, ZONES):
            perm = jnp.where(zones == i, table[i], perm)
        return perm * (h * h * h) / (1.0 + 2.0 * burden) * jnp.where(active, 0.001 + 0.999, 0.001)

    ylo, yhi = zero8, zero8
    for row in chunks:
        rows = slice(row, row + ROWS)
        at = slice(PAD + row, PAD + row + ROWS)
        height = th[rows, :]
        offset = jnp.zeros((ROWS, lanes), f32)
        total = tot[rows, :]
        for off in range(1, size["gz"]):
            piece = cs[off - 1, rows, :]
            lower = (me["gz"] >= off).astype(f32)
            offset = offset + piece * lower
            total = total + piece

        def kperm_step(z, carry):
            lo, hi = carry
            prefix = pre[z, rows, :] + offset
            heights[z, rows, :] = prefix / depth_total
            kp = permeability(
                zn[z + 1, rows, :], s[z + 1, at, :], (total - prefix) / depth_total, base + z < height
            )
            k[z + 1, at, :] = kp
            if row == 0:
                xs3[0, z] = kp[0:1, :]
            if row + ROWS == width:
                xs3[1, z] = kp[ROWS - 1:ROWS, :]
            for g in range(ROWS // 8):
                lo, hi = pack(kp[8 * g:8 * g + 8, :], z, row // 8 + g, lo, hi)
            return lo, hi

        ylo, yhi = lax.fori_loop(0, depth, kperm_step, (ylo, yhi))

        @pl.when(has("gz", 0))
        def _():
            k[0, at, :] = permeability(
                zn[0, rows, :], s[0, at, :], (total - offset) / depth_total, base - 1 < height
            )

        @pl.when(has("gz", 1))
        def _():
            st = s[depth + 1, at, :]
            active = base + depth < height
            prefix = offset + tot[rows, :] + jnp.where(active, 1.0 + st, 0.0)
            k[depth + 1, at, :] = permeability(
                zn[depth + 1, rows, :], st, (total - prefix) / depth_total, active
            )

    ys3[0], ys3[1] = yhi, ylo
    send(X3, "gx", *x3)
    send(Y3, "gy", *y3)

    receive(ZL, "gz", *zl)
    receive(X2, "gx", *x2)
    receive(Y2, "gy", *y2)

    def unpack_strain(z, carry):
        s[z + 1, PAD - 1:PAD, :] = xr2[0, z]
        s[z + 1, last:last + 1, :] = xr2[1, z]
        return carry

    lax.fori_loop(0, depth, unpack_strain, 0)

    for row in chunks:
        rows = slice(row, row + ROWS)
        at = slice(PAD + row, PAD + row + ROWS)
        packs = (yr2[0], yr2[1])

        def faces(z):
            ka, kb = k[z, at, :], k[z + 1, at, :]
            hh = 2.0 + s[z, at, :] + s[z + 1, at, :]
            twice = 2.0 / hh
            cond = 2.0 * twice * (ka * kb) / (ka + kb)
            fluxes = [twice * (u[c, z + 1, at, :] - u[c, z, at, :]) for c in range(3)]
            return fluxes, cond * (p[z + 1, at, :] - p[z, at, :])

        def vertical_step(z, carry):
            below, flow_below = carry
            above, flow_above = faces(z + 1)
            mid, xm, xp, ym, yp = shifts(s, packs, z, row)
            flow[z, rows, :] = flow_above - flow_below - mid
            grads = (xp - xm, yp - ym, s[z + 2, at, :] - s[z, at, :])
            for c in range(3):
                mech[c, z, rows, :] = mech[c, z, rows, :] + (above[c] - below[c]) + 0.25 * grads[c]
            return above, flow_above

        lax.fori_loop(0, depth, vertical_step, faces(0))

    receive(X3, "gx", *x3)
    receive(Y3, "gy", *y3)

    def unpack_kperm(z, carry):
        k[z + 1, PAD - 1:PAD, :] = xr3[0, z]
        k[z + 1, last:last + 1, :] = xr3[1, z]
        return carry

    lax.fori_loop(0, depth, unpack_kperm, 0)
    for row in chunks:
        rows = slice(row, row + ROWS)
        p_packs = (yr1[0, 3], yr1[1, 3])
        k_packs = (yr3[0], yr3[1])

        def flow_step(z, carry):
            ka, *ks = shifts(k, k_packs, z, row)
            pa, *ps = shifts(p, p_packs, z, row)
            out = flow[z, rows, :]
            twice = 2.0 * ka
            for kb, pb in zip(ks, ps):
                out = out + twice * kb / (ka + kb) * (pb - pa)
            flow[z, rows, :] = out
            return carry

        lax.fori_loop(0, depth, flow_step, 0)

    for message, axis, srcs, dsts in pending:
        for side in (0, 1):
            @pl.when(has(axis, side))
            def _():
                copy(message, axis, side, srcs[side], dsts[1 - side], side).wait_send()
    for off in range(1, size["gz"]):
        column(off, off).wait_send()


def local(counts, displacement, pressure, zone, perm_table, thickness):
    _, depth, width, lanes = displacement.shape
    f32 = jnp.float32
    tall = (depth + 2, width + 2 * PAD, lanes)
    row_face = lambda *lead: pltpu.VMEM((2, *lead, depth, 1, lanes), f32)
    lane_face = lambda *lead: pltpu.VMEM((2, *lead, 8, lanes), f32)
    hbm, vmem, smem = (pl.BlockSpec(memory_space=m) for m in (pl.ANY, pltpu.VMEM, pltpu.SMEM))
    others = max(counts[2] - 1, 1)
    return pl.pallas_call(
        functools.partial(kernel, counts),
        out_shape=(
            jax.ShapeDtypeStruct(pressure.shape, f32),
            jax.ShapeDtypeStruct(pressure.shape, f32),
            jax.ShapeDtypeStruct(displacement.shape, f32),
        ),
        in_specs=[hbm, hbm, hbm, smem, hbm],
        out_specs=(vmem, vmem, vmem),
        scratch_shapes=[
            pltpu.VMEM((3, *tall), f32),
            pltpu.VMEM(tall, f32),
            pltpu.VMEM(tall, f32),
            pltpu.VMEM(tall, f32),
            pltpu.VMEM((depth + 2, width, lanes), jnp.int32),
            pltpu.VMEM((width, lanes), jnp.int32),
            pltpu.VMEM((depth, width, lanes), f32),
            pltpu.VMEM((width, lanes), f32),
            row_face(4), row_face(4), lane_face(4), lane_face(4),
            row_face(), row_face(), lane_face(), lane_face(),
            row_face(), row_face(), lane_face(), lane_face(),
            pltpu.VMEM((others, width, lanes), f32),
            pltpu.SemaphoreType.DMA((6,)),
            pltpu.SemaphoreType.DMA((MESSAGES, 2)),
            pltpu.SemaphoreType.DMA((MESSAGES, 2)),
            pltpu.SemaphoreType.DMA((others,)),
            pltpu.SemaphoreType.DMA((others,)),
        ],
        compiler_params=pltpu.CompilerParams(
            collective_id=0, has_side_effects=True, vmem_limit_bytes=40 * 2**20
        ),
    )(displacement, pressure, zone, perm_table, thickness)


def solution(mesh):
    counts = tuple(mesh.shape[axis] for axis in AXES)
    in_specs = (
        P(None, "gz", "gx", "gy"),
        P("gz", "gx", "gy"),
        P("gz", "gx", "gy"),
        P(),
        P("gx", "gy"),
    )
    out_specs = (P("gz", "gx", "gy"), P("gz", "gx", "gy"), P(None, "gz", "gx", "gy"))
    return jax.shard_map(
        functools.partial(local, counts), mesh=mesh, in_specs=in_specs, out_specs=out_specs, check_vma=False
    )
```

time: 117 us -> 53.4 us (0.46)
  Pallas kernels: 0 us -> 44.8 us
  other arithmetic: 27.9 us -> 0 us
  starting transfers between devices: 25.4 us -> 0 us
  waiting for transfers between devices: 24.7 us -> 0 us
  local copies, waits for them, and re-layouts: 22.8 us -> 7.63 us
  blocking collectives: 13.7 us -> 0 us
    pallas_call x0 -> x1, Pallas kernels: none -> 44.8 us  [local(): pl.pallas_call(functools.partial(kernel, counts), out_shape=(jax.ShapeDty...]
    ppermute x12 -> x0, starting transfers between devices: 25.4 us -> none  [the longest x6 17.5 us: padded(): lax.ppermute(lax.slice_in_dim(block, block.shape[dim] - width, None, axis...]
    ppermute x12 -> x0, waiting for transfers between devices: 24.7 us -> none  [the longest x6 16.8 us: padded(): lax.ppermute(lax.slice_in_dim(block, 0, width, axis=dim), axis, backward)]
    all_gather x1 -> x0, blocking collectives: 13.7 us -> none  [column_sums(): pieces = lax.all_gather(column_local[None], 'gz', axis=0, tiled=True)]
    slice x9 -> x0, local copies, waits for them, and re-layouts: 12.8 us -> none  [the longest x5 7.87 us: padded(): lax.slice_in_dim(block, block.shape[dim] - width, None, axis=dim)]
    concatenate x4 -> x0, other arithmetic: 8.24 us -> none  [padded(): block = jnp.concatenate([low, block, high], axis=dim)]
    sub x2 -> x0, other arithmetic: 8.06 us -> none  [the longest x1 5.16 us: stencils(): mech = lateral + vertical + 0.5 * grads(strain_pad) - grads(press_pad)]
    another operation x3 -> x0, other arithmetic: 7.89 us -> none  [the longest x1 6.34 us: local(): state = jnp.stack([pressure, strain, kperm])]
  transfers between devices with their start and end apart: 12 -> 0, of which waited for: 9 -> 0; matrix products, arithmetic and copies ran while one was open for 7% -> 0% of each run, Pallas kernels for 0% -> 0%
where the time goes in v1:
time: 53.4 us; the launch traced here: 53.1 us
  Pallas kernels  44.8 us (84%)
  local copies, waits for them, and re-layouts  7.63 us (14%)
  between operations  0.65 us (1%)
    pallas_call x1, Pallas kernels, local(): pl.pallas_call(functools.partial(kernel, counts), out_shape=(jax.ShapeDty...  44.8 us
    unnamed x13, local copies, waits for them, and re-layouts  7.63 us

profile of v1, /device:TPU:0, one launch (start us, length us, event | category | flops | bytes accessed | tf_op | source)
XLA Modules:
  0.0 53.1 jit_solution(16627573158268229398)
XLA Ops:
  0.6 0.0 copy-start
  0.6 1.4 %copy-done = f32[3,16,64,128]{3,2,1,0:T(8,128)S(1)} copy-done((f32[3,16,64,128]{3,2,1,0:T(8,128)S(1)}, f32[3,16,64,128]{3,2,1,0:T(8,128)}, u32[]{:S(2)}) %copy-start) | copy-done | bytes 1572888
  2.0 0.0 copy-start.1
  2.0 1.0 %copy-done.1 = f32[16,64,128]{2,1,0:T(8,128)S(1)} copy-done((f32[16,64,128]{2,1,0:T(8,128)S(1)}, f32[16,64,128]{2,1,0:T(8,128)}, u32[]{:S(2)}) %copy-start.1) | copy-done | bytes 524312
  3.1 0.0 copy-start.2
  3.1 1.0 %copy-done.2 = s32[16,64,128]{2,1,0:T(8,128)S(1)} copy-done((s32[16,64,128]{2,1,0:T(8,128)S(1)}, s32[16,64,128]{2,1,0:T(8,128)}, u32[]{:S(2)}) %copy-start.2) | copy-done | bytes 524312
  4.1 0.0 copy-start.3
  4.1 0.8 %copy-done.3 = s32[64,128]{1,0:T(8,128)S(1)} copy-done((s32[64,128]{1,0:T(8,128)S(1)}, s32[64,128]{1,0:T(8,128)}, u32[]{:S(2)}) %copy-start.3) | copy-done | bytes 32792
  4.9 0.0 copy-start.4
  4.9 0.7 %copy-done.4 = f32[8]{0:T(128)S(1)} copy-done((f32[8]{0:T(128)S(1)}, f32[8]{0:T(128)}, u32[]{:S(2)}) %copy-start.4) | copy-done | bytes 56
  5.5 44.8 %shard_map.76 = (f32[16,64,128]{2,1,0:T(8,128)S(1)}, f32[16,64,128]{2,1,0:T(8,128)S(1)}, f32[3,16,64,128]{3,2,1,0:T(8,128)S(1)}) custom-call(f32[3,16,64,128]{3,2,1,0:T(8,128)S(1)} %copy-done, f32[16,64,128]{2,1,0:T(8,128)S(1)} %copy-done.1, s32[16,64,128]{2,1,0:T(8,128)S(1)} %copy-done.2, f32[8]{0:T(128)S(1)} %copy-done.4, s32[64,128]{1,0:T(8,128)S(1)} %copy-done.3), custom_call_target="tpu_custom_call" | custom-call | tf_op jit(solution)/shard_map/pallas_call | solution.py:396
  50.4 0.8 %copy.11 = f32[16,64,128]{2,1,0:T(8,128)} copy(f32[16,64,128]{2,1,0:T(8,128)S(1)} %get-tuple-element.6) | data formatting | bytes 1048576
  51.1 0.8 %copy.12 = f32[16,64,128]{2,1,0:T(8,128)} copy(f32[16,64,128]{2,1,0:T(8,128)S(1)} %get-tuple-element.7) | data formatting | bytes 1048576
  51.9 1.1 %copy.13 = f32[3,16,64,128]{3,2,1,0:T(8,128)} copy(f32[3,16,64,128]{3,2,1,0:T(8,128)S(1)} %get-tuple-element.8) | data formatting | bytes 3145728
Async XLA Ops:
  0.6 1.4 %copy-start = (f32[3,16,64,128]{3,2,1,0:T(8,128)S(1)}, f32[3,16,64,128]{3,2,1,0:T(8,128)}, u32[]{:S(2)}) copy-start(f32[3,16,64,128]{3,2,1,0:T(8,128)} %disp.1) | copy-start | bytes 4718596
  2.0 1.0 %copy-start.1 = (f32[16,64,128]{2,1,0:T(8,128)S(1)}, f32[16,64,128]{2,1,0:T(8,128)}, u32[]{:S(2)}) copy-start(f32[16,64,128]{2,1,0:T(8,128)} %press.1) | copy-start | bytes 1572868
  3.1 1.0 %copy-start.2 = (s32[16,64,128]{2,1,0:T(8,128)S(1)}, s32[16,64,128]{2,1,0:T(8,128)}, u32[]{:S(2)}) copy-start(s32[16,64,128]{2,1,0:T(8,128)} %zone.1) | copy-start | bytes 1572868
  4.1 0.8 %copy-start.3 = (s32[64,128]{1,0:T(8,128)S(1)}, s32[64,128]{1,0:T(8,128)}, u32[]{:S(2)}) copy-start(s32[64,128]{1,0:T(8,128)} %thick.1) | copy-start | bytes 98308
  4.9 0.7 %copy-start.4 = (f32[8]{0:T(128)S(1)}, f32[8]{0:T(128)}, u32[]{:S(2)}) copy-start(f32[8]{0:T(128)} %table.1) | copy-start | bytes 100

commit v2 on v1

--- a/solution.py
+++ b/solution.py
@@ -11,7 +11,8 @@
 ZONES = 8
 AXES = ("gx", "gy", "gz")
 PAD = 8
-ROWS = 16
+ROWS = 32
+UNROLL = 4
 
 X1, Y1, ZU, ZL, ZP, ZN, X2, Y2, ZS, X3, Y3 = range(11)
 MESSAGES = 11
@@ -148,7 +149,7 @@
             out += [lo, hi]
         return tuple(out)
 
-    accs = lax.fori_loop(0, depth, pack_inputs, (zero8,) * 8)
+    accs = lax.fori_loop(0, depth, pack_inputs, (zero8,) * 8, unroll=UNROLL)
     for i in range(4):
         ys1[0, i] = accs[2 * i + 1]
         ys1[1, i] = accs[2 * i]
@@ -177,7 +178,7 @@
             field[z + 1, last:last + 1, :] = xr1[1, i, z]
         return carry
 
-    lax.fori_loop(0, depth, unpack_inputs, 0)
+    lax.fori_loop(0, depth, unpack_inputs, 0, unroll=UNROLL)
 
     def shifts(field, packs, z, row):
         at = PAD + row
@@ -215,7 +216,7 @@
             pre[z, rows, :] = acc
             return acc, lo, hi
 
-        acc, ylo, yhi = lax.fori_loop(0, depth, strain_step, (jnp.zeros((ROWS, lanes), f32), ylo, yhi))
+        acc, ylo, yhi = lax.fori_loop(0, depth, strain_step, (jnp.zeros((ROWS, lanes), f32), ylo, yhi), unroll=UNROLL)
         tot[rows, :] = acc
     ys2[0], ys2[1] = yhi, ylo
 
@@ -249,7 +250,7 @@
                 mech[c, z, rows, :] = xp + xm + yp + ym - 4.0 * mid - 0.5 * grads[c]
             return carry
 
-        lax.fori_loop(0, depth, lateral_step, 0)
+        lax.fori_loop(0, depth, lateral_step, 0, unroll=UNROLL)
 
     loads[5].wait()
     for off in range(1, size["gz"]):
@@ -293,7 +294,7 @@
                 lo, hi = pack(kp[8 * g:8 * g + 8, :], z, row // 8 + g, lo, hi)
             return lo, hi
 
-        ylo, yhi = lax.fori_loop(0, depth, kperm_step, (ylo, yhi))
+        ylo, yhi = lax.fori_loop(0, depth, kperm_step, (ylo, yhi), unroll=UNROLL)
 
         @pl.when(has("gz", 0))
         def _():
@@ -323,7 +324,7 @@
         s[z + 1, last:last + 1, :] = xr2[1, z]
         return carry
 
-    lax.fori_loop(0, depth, unpack_strain, 0)
+    lax.fori_loop(0, depth, unpack_strain, 0, unroll=UNROLL)
 
     for row in chunks:
         rows = slice(row, row + ROWS)
@@ -348,7 +349,7 @@
                 mech[c, z, rows, :] = mech[c, z, rows, :] + (above[c] - below[c]) + 0.25 * grads[c]
             return above, flow_above
 
-        lax.fori_loop(0, depth, vertical_step, faces(0))
+        lax.fori_loop(0, depth, vertical_step, faces(0), unroll=UNROLL)
 
     receive(X3, "gx", *x3)
     receive(Y3, "gy", *y3)
@@ -358,7 +359,7 @@
         k[z + 1, last:last + 1, :] = xr3[1, z]
         return carry
 
-    lax.fori_loop(0, depth, unpack_kperm, 0)
+    lax.fori_loop(0, depth, unpack_kperm, 0, unroll=UNROLL)
     for row in chunks:
         rows = slice(row, row + ROWS)
         p_packs = (yr1[0, 3], yr1[1, 3])
@@ -374,7 +375,7 @@
             flow[z, rows, :] = out
             return carry
 
-        lax.fori_loop(0, depth, flow_step, 0)
+        lax.fori_loop(0, depth, flow_step, 0, unroll=UNROLL)
 
     for message, axis, srcs, dsts in pending:
         for side in (0, 1):
@@ -383,6 +384,15 @@
                 copy(message, axis, side, srcs[side], dsts[1 - side], side).wait_send()
     for off in range(1, size["gz"]):
         column(off, off).wait_send()
+
+
+def store(heights, flow, mech, heights_out, flow_out, mech_out, sem):
+    pairs = ((mech, mech_out), (heights, heights_out), (flow, flow_out))
+    copies = [pltpu.make_async_copy(src, dst, sem.at[i]) for i, (src, dst) in enumerate(pairs)]
+    for copy in copies:
+        copy.start()
+    for copy in copies:
+        copy.wait()
 
 
 def local(counts, displacement, pressure, zone, perm_table, thickness):
@@ -393,12 +403,16 @@
     lane_face = lambda *lead: pltpu.VMEM((2, *lead, 8, lanes), f32)
     hbm, vmem, smem = (pl.BlockSpec(memory_space=m) for m in (pl.ANY, pltpu.VMEM, pltpu.SMEM))
     others = max(counts[2] - 1, 1)
-    return pl.pallas_call(
+    inputs = [
+        pltpu.with_memory_space_constraint(x, pltpu.HBM)
+        for x in (displacement, pressure, zone, perm_table, thickness)
+    ]
+    fields = pl.pallas_call(
         functools.partial(kernel, counts),
         out_shape=(
-            jax.ShapeDtypeStruct(pressure.shape, f32),
-            jax.ShapeDtypeStruct(pressure.shape, f32),
-            jax.ShapeDtypeStruct(displacement.shape, f32),
+            pltpu.VMEM(pressure.shape, f32),
+            pltpu.VMEM(pressure.shape, f32),
+            pltpu.VMEM(displacement.shape, f32),
         ),
         in_specs=[hbm, hbm, hbm, smem, hbm],
         out_specs=(vmem, vmem, vmem),
@@ -424,7 +438,15 @@
         compiler_params=pltpu.CompilerParams(
             collective_id=0, has_side_effects=True, vmem_limit_bytes=40 * 2**20
         ),
-    )(displacement, pressure, zone, perm_table, thickness)
+    )(*inputs)
+    return pl.pallas_call(
+        store,
+        out_shape=tuple(jax.ShapeDtypeStruct(x.shape, f32) for x in (pressure, pressure, displacement)),
+        in_specs=[vmem] * 3,
+        out_specs=(hbm,) * 3,
+        scratch_shapes=[pltpu.SemaphoreType.DMA((3,))],
+        compiler_params=pltpu.CompilerParams(vmem_limit_bytes=2**20),
+    )(*[pltpu.with_memory_space_constraint(x, pltpu.VMEM) for x in fields])
 
 
 def solution(mesh):

time: 53.4 us -> 24.9 us (0.47)
  Pallas kernels: 44.8 us -> 24.1 us
  local copies, waits for them, and re-layouts: 7.63 us -> 0 us
    pallas_call x1 -> x2, Pallas kernels: 44.8 us -> 24.1 us  [the longest x1 22.6 us: local(): pl.pallas_call(functools.partial(kernel, counts), out_shape=(pltpu.VMEM(p...]
    unnamed x13 -> x0, local copies, waits for them, and re-layouts: 7.63 us -> none
where the time goes in v2:
time: 24.9 us; the launch traced here: 24.7 us
  Pallas kernels  24.1 us (97%)
  between operations  0.64 us (3%)
    pallas_call x1, Pallas kernels, local(): pl.pallas_call(functools.partial(kernel, counts), out_shape=(pltpu.VMEM(p...  22.6 us
    pallas_call x1, Pallas kernels, local(): pl.pallas_call(store, out_shape=tuple((jax.ShapeDtypeStruct(x.shape, f32)...  1.51 us

profile of v2, /device:TPU:0, one launch (start us, length us, event | category | flops | bytes accessed | tf_op | source)
XLA Modules:
  0.0 24.7 jit_solution(5841789682645399726)
XLA Ops:
  0.6 22.6 %shard_map.76 = (f32[16,64,128]{2,1,0:T(8,128)S(1)}, f32[16,64,128]{2,1,0:T(8,128)S(1)}, f32[3,16,64,128]{3,2,1,0:T(8,128)S(1)}) custom-call(f32[3,16,64,128]{3,2,1,0:T(8,128)} %disp.1, f32[16,64,128]{2,1,0:T(8,128)} %press.1, s32[16,64,128]{2,1,0:T(8,128)} %zone.1, f32[8]{0:T(128)} %table.1, s32[64,128]{1,0:T(8,128)} %thick.1), custom_call_target="tpu_custom_call" | custom-call | tf_op jit(solution)/shard_map/pallas_call | solution.py:410
  23.2 1.5 %shard_map.77 = (f32[16,64,128]{2,1,0:T(8,128)}, f32[16,64,128]{2,1,0:T(8,128)}, f32[3,16,64,128]{3,2,1,0:T(8,128)}) custom-call(f32[16,64,128]{2,1,0:T(8,128)S(1)} %get-tuple-element.6.heights, f32[16,64,128]{2,1,0:T(8,128)S(1)} %get-tuple-element.7.flow, f32[3,16,64,128]{3,2,1,0:T(8,128)S(1)} %get-tuple-element.8.mech), custom_call_target="tpu_custom_call" | custom-call | tf_op jit(solution)/shard_map/pallas_call | solution.py:442

commit v3 on v2

--- a/solution.py
+++ b/solution.py
@@ -122,6 +122,9 @@
         return lo, hi
 
     def yshift(v, packs, z, row):
+        if packs is None:
+            below = jnp.where(first_lane, 0.0, pltpu.roll(v, 1, 1))
+            return below, jnp.where(last_lane, 0.0, pltpu.roll(v, lanes - 1, 1))
         lo, hi = [], []
         lo_pack, hi_pack = packs
         for g in range(ROWS // 8):
@@ -176,6 +179,8 @@
         for i, field in enumerate(fields):
             field[z + 1, PAD - 1:PAD, :] = xr1[0, i, z]
             field[z + 1, last:last + 1, :] = xr1[1, i, z]
+        k[z + 1, PAD - 1:PAD, :] = jnp.zeros((1, lanes), f32)
+        k[z + 1, last:last + 1, :] = jnp.zeros((1, lanes), f32)
         return carry
 
     lax.fori_loop(0, depth, unpack_inputs, 0, unroll=UNROLL)
@@ -253,38 +258,51 @@
         lax.fori_loop(0, depth, lateral_step, 0, unroll=UNROLL)
 
     loads[5].wait()
-    for off in range(1, size["gz"]):
-        column(off, size["gz"] - off).wait_recv()
-    receive(ZS, "gz", *zs)
-    receive(ZN, "gz", *zz)
-
-    def permeability(zones, st, burden, active):
+
+    def unloaded(zones, st, active):
         h = 1.0 + st
         perm = jnp.full(zones.shape, table[0], f32)
         for i in range(1, ZONES):
             perm = jnp.where(zones == i, table[i], perm)
-        return perm * (h * h * h) / (1.0 + 2.0 * burden) * jnp.where(active, 0.001 + 0.999, 0.001)
-
-    ylo, yhi = zero8, zero8
+        return perm * (h * h * h) * jnp.where(active, 0.001 + 0.999, 0.001)
+
     for row in chunks:
         rows = slice(row, row + ROWS)
         at = slice(PAD + row, PAD + row + ROWS)
         height = th[rows, :]
+
+        def unloaded_step(z, carry):
+            k[z + 1, at, :] = unloaded(zn[z + 1, rows, :], s[z + 1, at, :], base + z < height)
+            return carry
+
+        lax.fori_loop(0, depth, unloaded_step, 0, unroll=UNROLL)
+
+    for off in range(1, size["gz"]):
+        column(off, size["gz"] - off).wait_recv()
+
+    def column_ends(rows):
         offset = jnp.zeros((ROWS, lanes), f32)
         total = tot[rows, :]
         for off in range(1, size["gz"]):
             piece = cs[off - 1, rows, :]
-            lower = (me["gz"] >= off).astype(f32)
-            offset = offset + piece * lower
+            offset = offset + piece * (me["gz"] >= off).astype(f32)
             total = total + piece
+        return offset, total
+
+    def permeability(free, burden):
+        return free / (1.0 + 2.0 * burden)
+
+    ylo, yhi = zero8, zero8
+    for row in chunks:
+        rows = slice(row, row + ROWS)
+        at = slice(PAD + row, PAD + row + ROWS)
+        offset, total = column_ends(rows)
 
         def kperm_step(z, carry):
             lo, hi = carry
             prefix = pre[z, rows, :] + offset
             heights[z, rows, :] = prefix / depth_total
-            kp = permeability(
-                zn[z + 1, rows, :], s[z + 1, at, :], (total - prefix) / depth_total, base + z < height
-            )
+            kp = permeability(k[z + 1, at, :], (total - prefix) / depth_total)
             k[z + 1, at, :] = kp
             if row == 0:
                 xs3[0, z] = kp[0:1, :]
@@ -296,24 +314,45 @@
 
         ylo, yhi = lax.fori_loop(0, depth, kperm_step, (ylo, yhi), unroll=UNROLL)
 
+    ys3[0], ys3[1] = yhi, ylo
+    send(X3, "gx", *x3)
+    send(Y3, "gy", *y3)
+
+    receive(ZS, "gz", *zs)
+    receive(ZN, "gz", *zz)
+    for row in chunks:
+        rows = slice(row, row + ROWS)
+        at = slice(PAD + row, PAD + row + ROWS)
+        height = th[rows, :]
+        offset, total = column_ends(rows)
+
         @pl.when(has("gz", 0))
         def _():
-            k[0, at, :] = permeability(
-                zn[0, rows, :], s[0, at, :], (total - offset) / depth_total, base - 1 < height
-            )
+            free = unloaded(zn[0, rows, :], s[0, at, :], base - 1 < height)
+            k[0, at, :] = permeability(free, (total - offset) / depth_total)
 
         @pl.when(has("gz", 1))
         def _():
             st = s[depth + 1, at, :]
             active = base + depth < height
             prefix = offset + tot[rows, :] + jnp.where(active, 1.0 + st, 0.0)
-            k[depth + 1, at, :] = permeability(
-                zn[depth + 1, rows, :], st, (total - prefix) / depth_total, active
-            )
-
-    ys3[0], ys3[1] = yhi, ylo
-    send(X3, "gx", *x3)
-    send(Y3, "gy", *y3)
+            free = unloaded(zn[depth + 1, rows, :], st, active)
+            k[depth + 1, at, :] = permeability(free, (total - prefix) / depth_total)
+
+    for row in chunks:
+        rows = slice(row, row + ROWS)
+
+        def flow_step(z, carry):
+            ka, *ks = shifts(k, None, z, row)
+            pa, *ps = shifts(p, None, z, row)
+            out = jnp.zeros((ROWS, lanes), f32)
+            twice = 2.0 * ka
+            for kb, pb in zip(ks, ps):
+                out = out + twice * kb / (ka + kb) * (pb - pa)
+            flow[z, rows, :] = out
+            return carry
+
+        lax.fori_loop(0, depth, flow_step, 0, unroll=UNROLL)
 
     receive(ZL, "gz", *zl)
     receive(X2, "gx", *x2)
@@ -343,7 +382,7 @@
             below, flow_below = carry
             above, flow_above = faces(z + 1)
             mid, xm, xp, ym, yp = shifts(s, packs, z, row)
-            flow[z, rows, :] = flow_above - flow_below - mid
+            flow[z, rows, :] = flow[z, rows, :] + (flow_above - flow_below) - mid
             grads = (xp - xm, yp - ym, s[z + 2, at, :] - s[z, at, :])
             for c in range(3):
                 mech[c, z, rows, :] = mech[c, z, rows, :] + (above[c] - below[c]) + 0.25 * grads[c]
@@ -354,28 +393,27 @@
     receive(X3, "gx", *x3)
     receive(Y3, "gy", *y3)
 
-    def unpack_kperm(z, carry):
-        k[z + 1, PAD - 1:PAD, :] = xr3[0, z]
-        k[z + 1, last:last + 1, :] = xr3[1, z]
+    def crossing(ka, kb, pa, pb):
+        return 2.0 * ka * kb / (ka + kb) * (pb - pa)
+
+    turn = lambda face: pltpu.roll(face, 1, 1)
+    side_lo = crossing(ys3[0], turn(yr3[0]), ys1[0, 3], turn(yr1[0, 3]))
+    side_hi = crossing(turn(ys3[1]), yr3[1], turn(ys1[1, 3]), yr1[1, 3])
+    first8, last8 = lane == 0, lane == lanes - 1
+
+    def sides_step(z, carry):
+        for side, row in ((0, 0), (1, width - 1)):
+            out = crossing(xs3[side, z], xr3[side, z], xs1[side, 3, z], xr1[side, 3, z])
+            flow[z, row:row + 1, :] = flow[z, row:row + 1, :] + out
+        for g in range(groups):
+            slot = z * groups + g
+            lo = pltpu.roll(side_lo, lax.rem(lanes - slot, lanes), 1)
+            hi = pltpu.roll(side_hi, lanes - 1 - slot, 1)
+            rows = slice(8 * g, 8 * g + 8)
+            flow[z, rows, :] = flow[z, rows, :] + jnp.where(first8, lo, jnp.where(last8, hi, 0.0))
         return carry
 
-    lax.fori_loop(0, depth, unpack_kperm, 0, unroll=UNROLL)
-    for row in chunks:
-        rows = slice(row, row + ROWS)
-        p_packs = (yr1[0, 3], yr1[1, 3])
-        k_packs = (yr3[0], yr3[1])
-
-        def flow_step(z, carry):
-            ka, *ks = shifts(k, k_packs, z, row)
-            pa, *ps = shifts(p, p_packs, z, row)
-            out = flow[z, rows, :]
-            twice = 2.0 * ka
-            for kb, pb in zip(ks, ps):
-                out = out + twice * kb / (ka + kb) * (pb - pa)
-            flow[z, rows, :] = out
-            return carry
-
-        lax.fori_loop(0, depth, flow_step, 0, unroll=UNROLL)
+    lax.fori_loop(0, depth, sides_step, 0, unroll=UNROLL)
 
     for message, axis, srcs, dsts in pending:
         for side in (0, 1):

time: 24.9 us -> 23 us (0.924)
  Pallas kernels: 24.1 us -> 22.2 us
    pallas_call x1, Pallas kernels: 22.6 us -> 20.7 us  [local(): pl.pallas_call(functools.partial(kernel, counts), out_shape=(pltpu.VMEM(p...]
where the time goes in v3:
time: 23 us; the launch traced here: 22.9 us
  Pallas kernels  22.2 us (97%)
  between operations  0.64 us (3%)
    pallas_call x1, Pallas kernels, local(): pl.pallas_call(functools.partial(kernel, counts), out_shape=(pltpu.VMEM(p...  20.7 us
    pallas_call x1, Pallas kernels, local(): pl.pallas_call(store, out_shape=tuple((jax.ShapeDtypeStruct(x.shape, f32)...  1.51 us

profile of v3, /device:TPU:0, one launch (start us, length us, event | category | flops | bytes accessed | tf_op | source)
XLA Modules:
  0.0 22.9 jit_solution(1719104754353355047)
XLA Ops:
  0.6 20.7 %shard_map.76 = (f32[16,64,128]{2,1,0:T(8,128)S(1)}, f32[16,64,128]{2,1,0:T(8,128)S(1)}, f32[3,16,64,128]{3,2,1,0:T(8,128)S(1)}) custom-call(f32[3,16,64,128]{3,2,1,0:T(8,128)} %disp.1, f32[16,64,128]{2,1,0:T(8,128)} %press.1, s32[16,64,128]{2,1,0:T(8,128)} %zone.1, f32[8]{0:T(128)} %table.1, s32[64,128]{1,0:T(8,128)} %thick.1), custom_call_target="tpu_custom_call" | custom-call | tf_op jit(solution)/shard_map/pallas_call | solution.py:448
  21.4 1.5 %shard_map.77 = (f32[16,64,128]{2,1,0:T(8,128)}, f32[16,64,128]{2,1,0:T(8,128)}, f32[3,16,64,128]{3,2,1,0:T(8,128)}) custom-call(f32[16,64,128]{2,1,0:T(8,128)S(1)} %get-tuple-element.6.heights, f32[16,64,128]{2,1,0:T(8,128)S(1)} %get-tuple-element.7.flow, f32[3,16,64,128]{3,2,1,0:T(8,128)S(1)} %get-tuple-element.8.mech), custom_call_target="tpu_custom_call" | custom-call | tf_op jit(solution)/shard_map/pallas_call | solution.py:480

commit v4 on v3

--- a/solution.py
+++ b/solution.py
@@ -12,15 +12,15 @@
 AXES = ("gx", "gy", "gz")
 PAD = 8
 ROWS = 32
-UNROLL = 4
-
-X1, Y1, ZU, ZL, ZP, ZN, X2, Y2, ZS, X3, Y3 = range(11)
-MESSAGES = 11
+UNROLL = 8
+
+X0, Y0, X1, Y1, ZU, ZL, ZP, ZN, X2, Y2, ZS, X3, Y3 = range(13)
+MESSAGES = 13
 
 
 def kernel(
     counts, disp, press, zone, table, thick, heights, flow, mech,
-    u, p, s, k, zn, th, pre, tot, xs1, xr1, ys1, yr1, xs2, xr2, ys2, yr2, xs3, xr3, ys3, yr3, cs,
+    u, p, s, k, zn, th, pre, tot, xs1, xr1, ys1, yr1, ysr, yrr, xs2, xr2, ys2, yr2, xs3, xr3, ys3, yr3, cs,
     load_sem, send_sem, recv_sem, col_send, col_recv,
 ):
     depth, width = disp.shape[1], disp.shape[2]
@@ -62,7 +62,6 @@
         pl.semaphore_signal(
             barrier, inc=1, device_id={"gz": lax.rem(me["gz"] + off, size["gz"])}, device_id_type=MESH
         )
-    pl.semaphore_wait(barrier, partners)
 
     pending = []
 
@@ -107,8 +106,6 @@
     zp = ((press.at[0], press.at[depth - 1]), (p.at[0, own], p.at[depth + 1, own]))
     zz = ((zone.at[0], zone.at[depth - 1]), (zn.at[0], zn.at[depth + 1]))
     zs = ((s.at[1, own], s.at[depth, own]), (s.at[0, own], s.at[depth + 1, own]))
-    send(ZU, "gz", *zu)
-
     lane = lax.broadcasted_iota(jnp.int32, (8, lanes), 1)
     lane_r = lax.broadcasted_iota(jnp.int32, (ROWS, lanes), 1)
     first_lane, last_lane = lane_r == 0, lane_r == lanes - 1
@@ -138,25 +135,50 @@
 
     fields = [u.at[0], u.at[1], u.at[2], p]
 
-    for load in loads[:4]:
-        load.wait()
+    def pack_first(z, carry):
+        lo, hi = carry
+        xs1[0, 0, z] = u[0, z + 1, PAD:PAD + 1, :]
+        xs1[1, 0, z] = u[0, z + 1, last - 1:last, :]
+        for g in range(groups):
+            lo, hi = pack(u[1, z + 1, PAD + 8 * g:PAD + 8 * g + 8, :], z, g, lo, hi)
+        return lo, hi
+
+    loads[0].wait()
+    loads[1].wait()
+    lo, hi = lax.fori_loop(0, depth, pack_first, (zero8,) * 2, unroll=UNROLL)
+    ys1[0] = hi
+    ys1[1] = lo
+
+    def part(ref, which):
+        return (ref.at[0, which], ref.at[1, which])
+
+    x0, y0 = (part(xs1, 0), part(xr1, 0)), (pair(ys1), pair(yr1))
+    x1, y1 = (part(xs1, pl.ds(1, 3)), part(xr1, pl.ds(1, 3))), (pair(ysr), pair(yrr))
+    pl.semaphore_wait(barrier, partners)
+    send(ZU, "gz", *zu)
+    send(X0, "gx", *x0)
+    send(Y0, "gy", *y0)
+
+    others = ((0, 0), (2, 1), (3, 2))
 
     def pack_inputs(z, accs):
         out = []
-        for i, field in enumerate(fields):
-            xs1[0, i, z] = field[z + 1, PAD:PAD + 1, :]
-            xs1[1, i, z] = field[z + 1, last - 1:last, :]
-            lo, hi = accs[2 * i:2 * i + 2]
+        for i in range(1, 4):
+            xs1[0, i, z] = fields[i][z + 1, PAD:PAD + 1, :]
+            xs1[1, i, z] = fields[i][z + 1, last - 1:last, :]
+        for i, n in others:
+            lo, hi = accs[2 * n:2 * n + 2]
             for g in range(groups):
-                lo, hi = pack(field[z + 1, PAD + 8 * g:PAD + 8 * g + 8, :], z, g, lo, hi)
+                lo, hi = pack(fields[i][z + 1, PAD + 8 * g:PAD + 8 * g + 8, :], z, g, lo, hi)
             out += [lo, hi]
         return tuple(out)
 
-    accs = lax.fori_loop(0, depth, pack_inputs, (zero8,) * 8, unroll=UNROLL)
-    for i in range(4):
-        ys1[0, i] = accs[2 * i + 1]
-        ys1[1, i] = accs[2 * i]
-    x1, y1 = (pair(xs1), pair(xr1)), (pair(ys1), pair(yr1))
+    loads[2].wait()
+    loads[3].wait()
+    accs = lax.fori_loop(0, depth, pack_inputs, (zero8,) * 6, unroll=UNROLL)
+    for i, n in others:
+        ysr[0, n] = accs[2 * n + 1]
+        ysr[1, n] = accs[2 * n]
     x2, y2 = (pair(xs2), pair(xr2)), (pair(ys2), pair(yr2))
     x3, y3 = (pair(xs3), pair(xr3)), (pair(ys3), pair(yr3))
     send(X1, "gx", *x1)
@@ -166,24 +188,29 @@
     send(ZN, "gz", *zz)
 
     clear("gx", [[xr.at[side] for xr in (xr1, xr2, xr3)] for side in (0, 1)])
-    clear("gy", [[yr.at[side] for yr in (yr1, yr2, yr3)] for side in (0, 1)])
+    clear("gy", [[yr.at[side] for yr in (yr1, yrr, yr2, yr3)] for side in (0, 1)])
     edges = (0, depth + 1)
     clear("gz", [[u.at[:, z, own], p.at[z, own], s.at[z, own], k.at[z, own], zn.at[z]] for z in edges])
     loads[4].wait()
 
     receive(ZU, "gz", *zu)
-    receive(X1, "gx", *x1)
-    receive(Y1, "gy", *y1)
+    receive(X0, "gx", *x0)
+    receive(Y0, "gy", *y0)
+
+    def unpack_first(z, carry):
+        u[0, z + 1, PAD - 1:PAD, :] = xr1[0, 0, z]
+        u[0, z + 1, last:last + 1, :] = xr1[1, 0, z]
+        return carry
+
+    lax.fori_loop(0, depth, unpack_first, 0, unroll=UNROLL)
 
     def unpack_inputs(z, carry):
-        for i, field in enumerate(fields):
-            field[z + 1, PAD - 1:PAD, :] = xr1[0, i, z]
-            field[z + 1, last:last + 1, :] = xr1[1, i, z]
+        for i in range(1, 4):
+            fields[i][z + 1, PAD - 1:PAD, :] = xr1[0, i, z]
+            fields[i][z + 1, last:last + 1, :] = xr1[1, i, z]
         k[z + 1, PAD - 1:PAD, :] = jnp.zeros((1, lanes), f32)
         k[z + 1, last:last + 1, :] = jnp.zeros((1, lanes), f32)
         return carry
-
-    lax.fori_loop(0, depth, unpack_inputs, 0, unroll=UNROLL)
 
     def shifts(field, packs, z, row):
         at = PAD + row
@@ -201,7 +228,7 @@
         rows = slice(row, row + ROWS)
         at = slice(PAD + row, PAD + row + ROWS)
         height = th[rows, :]
-        packs = (yr1[0, 1], yr1[1, 1])
+        packs = (yr1[0], yr1[1])
 
         def strain_step(z, carry):
             acc, lo, hi = carry
@@ -242,10 +269,13 @@
     send(ZS, "gz", *zs)
 
     receive(ZP, "gz", *zp)
+    receive(X1, "gx", *x1)
+    receive(Y1, "gy", *y1)
+    lax.fori_loop(0, depth, unpack_inputs, 0, unroll=UNROLL)
     for row in chunks:
         rows = slice(row, row + ROWS)
         at = slice(PAD + row, PAD + row + ROWS)
-        packs = [(yr1[0, i], yr1[1, i]) for i in range(4)]
+        packs = [(yrr[0, 0], yrr[1, 0]), (yr1[0], yr1[1]), (yrr[0, 1], yrr[1, 1]), (yrr[0, 2], yrr[1, 2])]
 
         def lateral_step(z, carry):
             _, xm, xp, ym, yp = shifts(p, packs[3], z, row)
@@ -397,8 +427,8 @@
         return 2.0 * ka * kb / (ka + kb) * (pb - pa)
 
     turn = lambda face: pltpu.roll(face, 1, 1)
-    side_lo = crossing(ys3[0], turn(yr3[0]), ys1[0, 3], turn(yr1[0, 3]))
-    side_hi = crossing(turn(ys3[1]), yr3[1], turn(ys1[1, 3]), yr1[1, 3])
+    side_lo = crossing(ys3[0], turn(yr3[0]), ysr[0, 2], turn(yrr[0, 2]))
+    side_hi = crossing(turn(ys3[1]), yr3[1], turn(ysr[1, 2]), yrr[1, 2])
     first8, last8 = lane == 0, lane == lanes - 1
 
     def sides_step(z, carry):
@@ -463,7 +493,7 @@
             pltpu.VMEM((width, lanes), jnp.int32),
             pltpu.VMEM((depth, width, lanes), f32),
             pltpu.VMEM((width, lanes), f32),
-            row_face(4), row_face(4), lane_face(4), lane_face(4),
+            row_face(4), row_face(4), lane_face(), lane_face(), lane_face(3), lane_face(3),
             row_face(), row_face(), lane_face(), lane_face(),
             row_face(), row_face(), lane_face(), lane_face(),
             pltpu.VMEM((others, width, lanes), f32),

time: 23 us -> 21.7 us (0.943)
  Pallas kernels: 22.2 us -> 20.9 us
    pallas_call x1, Pallas kernels: 20.7 us -> 19.4 us  [local(): pl.pallas_call(functools.partial(kernel, counts), out_shape=(pltpu.VMEM(p...]
where the time goes in v4:
time: 21.7 us; the launch traced here: 21.5 us
  Pallas kernels  20.9 us (96%)
  between operations  0.64 us (3%)
    pallas_call x1, Pallas kernels, local(): pl.pallas_call(functools.partial(kernel, counts), out_shape=(pltpu.VMEM(p...  19.4 us
    pallas_call x1, Pallas kernels, local(): pl.pallas_call(store, out_shape=tuple((jax.ShapeDtypeStruct(x.shape, f32)...  1.51 us

profile of v4, /device:TPU:0, one launch (start us, length us, event | category | flops | bytes accessed | tf_op | source)
XLA Modules:
  0.0 21.5 jit_solution(259098335086961494)
XLA Ops:
  0.6 19.4 %shard_map.76 = (f32[16,64,128]{2,1,0:T(8,128)S(1)}, f32[16,64,128]{2,1,0:T(8,128)S(1)}, f32[3,16,64,128]{3,2,1,0:T(8,128)S(1)}) custom-call(f32[3,16,64,128]{3,2,1,0:T(8,128)} %disp.1, f32[16,64,128]{2,1,0:T(8,128)} %press.1, s32[16,64,128]{2,1,0:T(8,128)} %zone.1, f32[8]{0:T(128)} %table.1, s32[64,128]{1,0:T(8,128)} %thick.1), custom_call_target="tpu_custom_call" | custom-call | tf_op jit(solution)/shard_map/pallas_call | solution.py:478
  20.0 1.5 %shard_map.77 = (f32[16,64,128]{2,1,0:T(8,128)}, f32[16,64,128]{2,1,0:T(8,128)}, f32[3,16,64,128]{3,2,1,0:T(8,128)}) custom-call(f32[16,64,128]{2,1,0:T(8,128)S(1)} %get-tuple-element.6.heights, f32[16,64,128]{2,1,0:T(8,128)S(1)} %get-tuple-element.7.flow, f32[3,16,64,128]{3,2,1,0:T(8,128)S(1)} %get-tuple-element.8.mech), custom_call_target="tpu_custom_call" | custom-call | tf_op jit(solution)/shard_map/pallas_call | solution.py:510

commit v5 on v4

--- a/solution.py
+++ b/solution.py
@@ -19,7 +19,7 @@
 
 
 def kernel(
-    counts, disp, press, zone, table, thick, heights, flow, mech,
+    counts, disp, press, zone, table, thick, heights, flow, mech, lane_sides, row_sides,
     u, p, s, k, zn, th, pre, tot, xs1, xr1, ys1, yr1, ysr, yrr, xs2, xr2, ys2, yr2, xs3, xr3, ys3, yr3, cs,
     load_sem, send_sem, recv_sem, col_send, col_recv,
 ):
@@ -427,20 +427,12 @@
         return 2.0 * ka * kb / (ka + kb) * (pb - pa)
 
     turn = lambda face: pltpu.roll(face, 1, 1)
-    side_lo = crossing(ys3[0], turn(yr3[0]), ysr[0, 2], turn(yrr[0, 2]))
-    side_hi = crossing(turn(ys3[1]), yr3[1], turn(ysr[1, 2]), yrr[1, 2])
-    first8, last8 = lane == 0, lane == lanes - 1
+    lane_sides[0] = crossing(ys3[0], turn(yr3[0]), ysr[0, 2], turn(yrr[0, 2]))
+    lane_sides[1] = crossing(turn(ys3[1]), yr3[1], turn(ysr[1, 2]), yrr[1, 2])
 
     def sides_step(z, carry):
-        for side, row in ((0, 0), (1, width - 1)):
-            out = crossing(xs3[side, z], xr3[side, z], xs1[side, 3, z], xr1[side, 3, z])
-            flow[z, row:row + 1, :] = flow[z, row:row + 1, :] + out
-        for g in range(groups):
-            slot = z * groups + g
-            lo = pltpu.roll(side_lo, lax.rem(lanes - slot, lanes), 1)
-            hi = pltpu.roll(side_hi, lanes - 1 - slot, 1)
-            rows = slice(8 * g, 8 * g + 8)
-            flow[z, rows, :] = flow[z, rows, :] + jnp.where(first8, lo, jnp.where(last8, hi, 0.0))
+        for side in (0, 1):
+            row_sides[side, z] = crossing(xs3[side, z], xr3[side, z], xs1[side, 3, z], xr1[side, 3, z])
         return carry
 
     lax.fori_loop(0, depth, sides_step, 0, unroll=UNROLL)
@@ -454,11 +446,37 @@
         column(off, off).wait_send()
 
 
-def store(heights, flow, mech, heights_out, flow_out, mech_out, sem):
-    pairs = ((mech, mech_out), (heights, heights_out), (flow, flow_out))
-    copies = [pltpu.make_async_copy(src, dst, sem.at[i]) for i, (src, dst) in enumerate(pairs)]
+def store(heights, flow, mech, lane_sides, row_sides, heights_out, flow_out, mech_out, whole, sem):
+    depth, width, lanes = whole.shape
+    groups = width // 8
+    copies = [
+        pltpu.make_async_copy(mech, mech_out, sem.at[0]),
+        pltpu.make_async_copy(heights, heights_out, sem.at[1]),
+    ]
     for copy in copies:
         copy.start()
+    lane = lax.broadcasted_iota(jnp.int32, (8, lanes), 1)
+    first, last = lane == 0, lane == lanes - 1
+    side_lo, side_hi = lane_sides[0], lane_sides[1]
+
+    def step(z, carry):
+        for g in range(groups):
+            slot = z * groups + g
+            lo = pltpu.roll(side_lo, lax.rem(lanes - slot, lanes), 1)
+            hi = pltpu.roll(side_hi, lanes - 1 - slot, 1)
+            rows = slice(8 * g, 8 * g + 8)
+            whole[z, rows, :] = flow[z, rows, :] + jnp.where(first, lo, jnp.where(last, hi, 0.0))
+        for side, row in ((0, 0), (1, width - 1)):
+            whole[z, row:row + 1, :] = whole[z, row:row + 1, :] + row_sides[side, z]
+        return carry
+
+    half = depth // 2
+    for part in range(2):
+        lax.fori_loop(part * half, (part + 1) * half, step, 0, unroll=4)
+        layers = pl.ds(part * half, half)
+        copy = pltpu.make_async_copy(whole.at[layers], flow_out.at[layers], sem.at[2 + part])
+        copy.start()
+        copies.append(copy)
     for copy in copies:
         copy.wait()
 
@@ -481,9 +499,11 @@
             pltpu.VMEM(pressure.shape, f32),
             pltpu.VMEM(pressure.shape, f32),
             pltpu.VMEM(displacement.shape, f32),
+            pltpu.VMEM((2, 8, lanes), f32),
+            pltpu.VMEM((2, depth, 1, lanes), f32),
         ),
         in_specs=[hbm, hbm, hbm, smem, hbm],
-        out_specs=(vmem, vmem, vmem),
+        out_specs=(vmem,) * 5,
         scratch_shapes=[
             pltpu.VMEM((3, *tall), f32),
             pltpu.VMEM(tall, f32),
@@ -510,10 +530,10 @@
     return pl.pallas_call(
         store,
         out_shape=tuple(jax.ShapeDtypeStruct(x.shape, f32) for x in (pressure, pressure, displacement)),
-        in_specs=[vmem] * 3,
+        in_specs=[vmem] * 5,
         out_specs=(hbm,) * 3,
-        scratch_shapes=[pltpu.SemaphoreType.DMA((3,))],
-        compiler_params=pltpu.CompilerParams(vmem_limit_bytes=2**20),
+        scratch_shapes=[pltpu.VMEM(pressure.shape, f32), pltpu.SemaphoreType.DMA((4,))],
+        compiler_params=pltpu.CompilerParams(vmem_limit_bytes=4 * 2**20),
     )(*[pltpu.with_memory_space_constraint(x, pltpu.VMEM) for x in fields])
 
 

time: 21.7 us -> 21.3 us (0.982)
  Pallas kernels: 20.9 us -> 20.5 us
    pallas_call x1, Pallas kernels: 19.4 us -> 18.9 us  [local(): pl.pallas_call(functools.partial(kernel, counts), out_shape=(pltpu.VMEM(p...]
where the time goes in v5:
time: 21.3 us; the launch traced here: 21.1 us
  Pallas kernels  20.5 us (96%)
  between operations  0.64 us (3%)
    pallas_call x1, Pallas kernels, local(): pl.pallas_call(functools.partial(kernel, counts), out_shape=(pltpu.VMEM(p...  18.9 us
    pallas_call x1, Pallas kernels, local(): pl.pallas_call(store, out_shape=tuple((jax.ShapeDtypeStruct(x.shape, f32)...  1.52 us

profile of v5, /device:TPU:0, one launch (start us, length us, event | category | flops | bytes accessed | tf_op | source)
XLA Modules:
  0.0 21.1 jit_solution(2882683082151541558)
XLA Ops:
  0.6 18.9 %shard_map.76 = (f32[16,64,128]{2,1,0:T(8,128)S(1)}, f32[16,64,128]{2,1,0:T(8,128)S(1)}, f32[3,16,64,128]{3,2,1,0:T(8,128)S(1)}, f32[2,8,128]{2,1,0:T(8,128)S(1)}, f32[2,16,1,128]{3,2,1,0:T(1,128)S(1)}) custom-call(f32[3,16,64,128]{3,2,1,0:T(8,128)} %disp.1, f32[16,64,128]{2,1,0:T(8,128)} %press.1, s32[16,64,128]{2,1,0:T(8,128)} %zone.1, f32[8]{0:T(128)} %table.1, ...), custom_call_target="tpu_custom_call" | custom-call | tf_op jit(solution)/shard_map/pallas_call | solution.py:496
  19.6 1.5 %shard_map.77 = (f32[16,64,128]{2,1,0:T(8,128)}, f32[16,64,128]{2,1,0:T(8,128)}, f32[3,16,64,128]{3,2,1,0:T(8,128)}) custom-call(f32[16,64,128]{2,1,0:T(8,128)S(1)} %get-tuple-element.8.heights, f32[16,64,128]{2,1,0:T(8,128)S(1)} %get-tuple-element.9.flow, f32[3,16,64,128]{3,2,1,0:T(8,128)S(1)} %get-tuple-element.10.mech, ...), custom_call_target="tpu_custom_call" | custom-call | tf_op jit(solution)/shard_map/pallas_call | solution.py:530
